TPU v7x, 128 devices: a whole 4x4x4 slice. The times are simulated.
128 devices in a mesh: sub: 16 (over z, x), grp: 8 (over y, core).
Axes of the slice: x: 4, y: 4, z: 4, core: 2. Of those that a mesh axis runs over, the one named last changes fastest.
Arguments:
- rhs: float32 [8, 64, 256, 256], P('grp', 'sub')
- counts: int32 [8, 64], P('grp', 'sub'), may hold values from 64 to 256, as said below
- solve_panel: bfloat16 [8, 64, 512, 512], P('grp', 'sub'), as said below
- dirichlet_panel: bfloat16 [8, 64, 512, 512], P('grp', 'sub'), as said below
- coupling: float32 [8, 64, 32, 512], P('grp', 'sub'), may hold values from -0.25 to 0.25
- corner_map: int32 [8, 64, 32], P('grp', 'sub'), may hold values from 0 to 2047
- coarse_inverse: float32 [16, 2048, 2048], P('sub', 'grp'), as said below
Outputs:
- multipliers: float32 [8, 64, 256, 256], P('grp', 'sub')
- residual: float32 [8, 64, 256, 256], P('grp', 'sub')
Inputs may be any that keep to these rules, and one draw needn't show every extreme that they name: `counts`: some pair has all 256 unknowns constrained. `solve_panel`: each panel is symmetric positive definite. `dirichlet_panel`: each panel is symmetric positive definite. `coarse_inverse`: each slab's matrix is symmetric positive definite.
All inputs are finite; a program needn't handle non-finite values.
Results may differ from a plain program's by a relative error of at most 0.0003.
Values sent between devices are 32-bit elements; how exact they have to be, the bound alone decides.
A program may use at most 128 MiB of HBM per device.

v0:
```python
import jax
import jax.numpy as jnp
from jax import lax
from jax.sharding import PartitionSpec as P

ITERS = 3
HIGH = lax.Precision.HIGHEST


def passed_along(block, axis, distance):
    devices = range(lax.axis_size(axis))
    route = [(i - distance, i) for i in devices if i - distance in devices]
    return lax.ppermute(block, axis, route)


def spread_faces(values):
    previous = passed_along(values[:, -1:], "sub", 1)
    prior = jnp.concatenate([previous, values[:, :-1]], axis=1)
    return jnp.concatenate([-prior, values], axis=3)


def face_jump(result, live_mask):
    width = result.shape[3] // 2
    following = passed_along(result[:, :1, :, :width], "sub", -1)
    next_left = jnp.concatenate([result[:, 1:, :, :width], following], axis=1)
    return live_mask * (result[..., width:] - next_left)


def panel_apply(panel, face_vals):
    return jnp.einsum(
        "gsrp,gsqp->gsrq", face_vals, panel, precision=HIGH, preferred_element_type=jnp.float32
    )


def inner(first, second):
    return jnp.sum(first * second, axis=(0, 1, 3))


def expand(scalars):
    return scalars[None, None, :, None]


def residual_sum(resid, precond):
    return lax.psum(inner(resid, precond), ("sub", "grp"))


def local(rhs, counts, solve_panel, dirichlet_panel, coupling, corner_map, coarse_inverse):
    local_subs = rhs.shape[1]
    width = rhs.shape[3]
    size = coarse_inverse.shape[2]
    last_device = lax.axis_index("sub") == lax.axis_size("sub") - 1
    slots = jnp.arange(local_subs, dtype=jnp.int32)
    positions = jnp.arange(width, dtype=jnp.int32)
    not_last = jnp.logical_not(last_device & (slots == local_subs - 1))
    live = (positions[None, None, :] < counts[:, :, None]) & not_last[None, :, None]
    live_mask = live.astype(jnp.float32)[:, :, None, :]
    corner_onehot = (corner_map[0][..., None] == jnp.arange(size, dtype=jnp.int32)).astype(
        jnp.float32
    )

    def precondition(values):
        return 0.25 * face_jump(panel_apply(dirichlet_panel, spread_faces(values)), live_mask)

    multipliers = jnp.zeros_like(rhs)
    residual = live_mask * rhs
    precond = precondition(residual)
    direction = precond
    rz_now = residual_sum(residual, precond)
    for step in range(ITERS):
        apply_face_vals = spread_faces(direction)
        corner_vals = jnp.einsum("srp,skp->srk", apply_face_vals[0], coupling[0], precision=HIGH)
        owned_totals = lax.psum_scatter(
            jnp.einsum("skn,srk->nr", corner_onehot, corner_vals, precision=HIGH),
            "grp",
            scatter_dimension=0,
            tiled=True,
        )
        partial_solved = jnp.einsum("mn,mr->nr", coarse_inverse[0], owned_totals, precision=HIGH)
        solved = lax.psum(partial_solved, "grp")
        back = jnp.einsum("skn,nr->srk", corner_onehot, solved, precision=HIGH)
        result = (
            panel_apply(solve_panel, apply_face_vals)
            + jnp.einsum("srk,skp->srp", back, coupling[0], precision=HIGH)[None]
        )
        image = face_jump(result, live_mask)
        alpha = rz_now / lax.psum(inner(direction, image), ("sub", "grp"))
        multipliers = multipliers + expand(alpha) * direction
        residual = residual - expand(alpha) * image
        if step + 1 < ITERS:
            precond = precondition(residual)
            rz_next = residual_sum(residual, precond)
            direction = precond + expand(rz_next / rz_now) * direction
            rz_now = rz_next
    return (multipliers, residual)


def solution(mesh):
    return jax.shard_map(
        local,
        mesh=mesh,
        in_specs=(
            P("grp", "sub", None, None),
            P("grp", "sub"),
            P("grp", "sub", None, None),
            P("grp", "sub", None, None),
            P("grp", "sub", None, None),
            P("grp", "sub", None),
            P("sub", "grp", None),
        ),
        out_specs=(P("grp", "sub", None, None), P("grp", "sub", None, None)),
        check_vma=False,
    )
```

profile of v0, /device:TPU:1, one launch (start us, length us, event | category | flops | bytes accessed | tf_op | source)
XLA Modules:
  0.0 832.8 jit_solution(642383770802080915)
XLA Ops:
  13.5 4.9 collective-permute-done
  21.7 7.8 collective-permute-done.1
  42.0 38.6 %reduce-scatter.4.cloned.1.call-done = f32[256,256]{1,0:T(8,128)} async-done(((f32[2048,256]{1,0:T(8,128)}), f32[256,256]{1,0:T(8,128)}) %reduce-scatter.4.cloned.1.call-update) | async-done | bytes 262160 | tf_op jit(solution)/shard_map/reduce_scatter | solution.py:72
  80.6 4.9 convolution_bitcast_fusion.5
  85.8 65.4 %all-reduce.5.cloned.1.call-done = f32[2048,256]{0,1:T(8,128)} async-done(((f32[2048,256]{0,1:T(8,128)}), f32[2048,256]{0,1:T(8,128)}) %all-reduce.5.cloned.1.call-update) | async-done | bytes 2097168 | tf_op jit(solution)/shard_map/psum | solution.py:79
  159.7 5.7 collective-permute-done.3
  166.2 70.6 %all-reduce = (f32[256]{0:T(256)S(1)}, f32[256]{0:T(256)S(1)}) all-reduce(f32[256]{0:T(256)S(1)} %get-tuple-element.3, f32[256]{0:T(256)S(1)} %get-tuple-element.2), channel_id=1, replica_groups=mesh['sub'=16,'grp'=8] {'sub','grp'}, use_global_device_ids=true, to_apply=%region_1.0 | all-reduce | flops 512 | bytes 4096 | tf_op jit(solution)/shard_map/psum | solution.py:44
  241.4 4.6 collective-permute-done.4
  249.4 7.5 collective-permute-done.5
  258.0 67.7 %psum.66 = f32[256]{0:T(256)S(1)} all-reduce(f32[256]{0:T(256)S(1)} %multiply_reduce_fusion.3), channel_id=1, replica_groups=mesh['sub'=16,'grp'=8] {'sub','grp'}, use_global_device_ids=true, to_apply=%region_7.0 | all-reduce | flops 256 | bytes 2048 | tf_op jit(solution)/shard_map/psum | solution.py:44
  341.7 32.0 %reduce-scatter.6.cloned.1.call-done = f32[256,256]{1,0:T(8,128)} async-done(((f32[2048,256]{1,0:T(8,128)}), f32[256,256]{1,0:T(8,128)}) %reduce-scatter.6.cloned.1.call-update) | async-done | bytes 262160 | tf_op jit(solution)/shard_map/reduce_scatter | solution.py:72
  373.7 4.9 convolution_bitcast_fusion.4
  378.7 65.6 %all-reduce.7.cloned.1.call-done = f32[2048,256]{0,1:T(8,128)} async-done(((f32[2048,256]{0,1:T(8,128)}), f32[2048,256]{0,1:T(8,128)}) %all-reduce.7.cloned.1.call-update) | async-done | bytes 2097168 | tf_op jit(solution)/shard_map/psum | solution.py:79
  452.6 5.7 collective-permute-done.7
  459.4 71.1 %psum.68 = f32[256]{0:T(256)S(1)} all-reduce(f32[256]{0:T(256)S(1)} %multiply_reduce_fusion.2), channel_id=1, replica_groups=mesh['sub'=16,'grp'=8] {'sub','grp'}, use_global_device_ids=true, to_apply=%region_11.0 | all-reduce | flops 256 | bytes 2048 | tf_op jit(solution)/shard_map/psum | solution.py:86
  535.1 4.6 collective-permute-done.8
  543.0 7.5 collective-permute-done.9
  551.6 67.7 %psum.69 = f32[256]{0:T(256)S(1)} all-reduce(f32[256]{0:T(256)S(1)} %multiply_reduce_fusion.1), channel_id=1, replica_groups=mesh['sub'=16,'grp'=8] {'sub','grp'}, use_global_device_ids=true, to_apply=%region_13.0 | all-reduce | flops 256 | bytes 2048 | tf_op jit(solution)/shard_map/psum | solution.py:44
  623.6 4.8 collective-permute-done.10
  634.3 31.8 %reduce-scatter.8.cloned.1.call-done = f32[256,256]{1,0:T(8,128)} async-done(((f32[2048,256]{1,0:T(8,128)}), f32[256,256]{1,0:T(8,128)}) %reduce-scatter.8.cloned.1.call-update) | async-done | bytes 262160 | tf_op jit(solution)/shard_map/reduce_scatter | solution.py:72
  666.1 4.9 convolution_bitcast_fusion.3
  671.0 65.7 %all-reduce.9.cloned.1.call-done = f32[2048,256]{0,1:T(8,128)} async-done(((f32[2048,256]{0,1:T(8,128)}), f32[2048,256]{0,1:T(8,128)}) %all-reduce.9.cloned.1.call-update) | async-done | bytes 2097168 | tf_op jit(solution)/shard_map/psum | solution.py:79
  744.9 5.7 collective-permute-done.11
  750.9 70.7 %psum.71 = f32[256]{0:T(256)S(1)} all-reduce(f32[256]{0:T(256)S(1)} %multiply_reduce_fusion), channel_id=1, replica_groups=mesh['sub'=16,'grp'=8] {'sub','grp'}, use_global_device_ids=true, to_apply=%region_17.0 | all-reduce | flops 256 | bytes 2048 | tf_op jit(solution)/shard_map/psum | solution.py:86
  (161 shorter events, 97.1 us)
Async XLA Ops:
  7.2 11.3 %copy-start = (bf16[1,4,512,512]{3,2,1,0:T(8,128)(2,1)S(1)}, bf16[1,4,512,512]{3,2,1,0:T(8,128)(2,1)}, u32[]{:S(2)}) copy-start(bf16[1,4,512,512]{3,2,1,0:T(8,128)(2,1)} %param.10) | copy-start | bytes 6291460
  7.2 73.4 %reduce-scatter.4.cloned.1.call-start = ((), (), s32[]{:S(2)}) async-start(), calls=%async_computation.3 | async-start | bytes 2359296 | tf_op jit(solution)/shard_map/reduce_scatter | solution.py:72
  9.4 8.9 %collective-permute-start = (f32[1,1,256,256]{3,2,1,0:T(8,128)S(1)}, f32[1,1,256,256]{3,2,1,0:T(8,128)S(1)}, u32[]{:S(2)}, u32[]{:S(2)}) collective-permute-start(f32[1,1,256,256]{3,2,1,0:T(8,128)S(1)} %slice.120), channel_id=1, source_target_pairs={{0,8},{8,16},{16,24},{24,32},{32,40},{40,48},{48,56},{56,64},{64,7... | collective-permute-start | bytes 786440 | tf_op jit(solution)/shard_map/ppermute | solution.py:13
  20.3 9.2 %collective-permute-start.1 = (f32[1,1,256,256]{3,2,1,0:T(8,128)S(1)}, f32[1,1,256,256]{3,2,1,0:T(8,128)S(1)}, u32[]{:S(2)}, u32[]{:S(2)}) collective-permute-start(f32[1,1,256,256]{3,2,1,0:T(8,128)S(1)} %slice.124), channel_id=1, source_target_pairs={{8,0},{16,8},{24,16},{32,24},{40,32},{48,40},{56,48},{64,56},{72,6... | collective-permute-start | bytes 786440 | tf_op jit(solution)/shard_map/ppermute | solution.py:13
  29.7 135.8 %copy-start.8 = (f32[1,4,256,256]{3,2,1,0:T(8,128)}, f32[1,4,256,256]{3,2,1,0:T(8,128)S(1)}, u32[]{:S(2)}) copy-start(f32[1,4,256,256]{3,2,1,0:T(8,128)S(1)} %get-tuple-element.9) | copy-start | bytes 3145732
  29.7 6.5 collective-permute-start.2
  42.0 109.2 %all-reduce.5.cloned.1.call-start = ((), (), s32[]{:S(2)}) async-start(), calls=%async_computation.4 | async-start | bytes 4194304 | tf_op jit(solution)/shard_map/psum | solution.py:79
  85.5 288.2 %reduce-scatter.6.cloned.1.call-start = ((), (), s32[]{:S(2)}) async-start(), calls=%async_computation.5 | async-start | bytes 2359296 | tf_op jit(solution)/shard_map/reduce_scatter | solution.py:72
  158.1 7.4 collective-permute-start.3
  238.9 18.0 %copy-start.4 = (f32[1,4,256,256]{3,2,1,0:T(8,128)}, f32[1,4,256,256]{3,2,1,0:T(8,128)S(1)}, u32[]{:S(2)}) copy-start(f32[1,4,256,256]{3,2,1,0:T(8,128)S(1)} %multiply_subtract_fusion.2) | copy-start | bytes 3145732
  238.9 7.1 collective-permute-start.4
  248.0 8.9 %copy-start.11 = (f32[1,4,256,512]{3,2,1,0:T(8,128)}, f32[1,4,256,512]{3,2,1,0:T(8,128)S(1)}, u32[]{:S(2)}) copy-start(f32[1,4,256,512]{3,2,1,0:T(8,128)S(1)} %fusion.39) | copy-start | bytes 6291460
  248.0 8.9 %collective-permute-start.5 = (f32[1,1,256,256]{3,2,1,0:T(8,128)S(1)}, f32[1,1,256,256]{3,2,1,0:T(8,128)S(1)}, u32[]{:S(2)}, u32[]{:S(2)}) collective-permute-start(f32[1,1,256,256]{3,2,1,0:T(8,128)S(1)} %slice.134), channel_id=1, source_target_pairs={{8,0},{16,8},{24,16},{32,24},{40,32},{48,40},{56,48},{64,56},{72,6... | collective-permute-start | bytes 786440 | tf_op jit(solution)/shard_map/ppermute | solution.py:13
  327.8 7.2 collective-permute-start.6
  341.7 102.7 %all-reduce.7.cloned.1.call-start = ((), (), s32[]{:S(2)}) async-start(), calls=%async_computation.6 | async-start | bytes 4194304 | tf_op jit(solution)/shard_map/psum | solution.py:79
  378.7 287.4 %reduce-scatter.8.cloned.1.call-start = ((), (), s32[]{:S(2)}) async-start(), calls=%async_computation.7 | async-start | bytes 2359296 | tf_op jit(solution)/shard_map/reduce_scatter | solution.py:72
  451.2 7.1 collective-permute-start.7
  532.5 18.0 %copy-start.3 = (f32[1,4,256,256]{3,2,1,0:T(8,128)}, f32[1,4,256,256]{3,2,1,0:T(8,128)S(1)}, u32[]{:S(2)}) copy-start(f32[1,4,256,256]{3,2,1,0:T(8,128)S(1)} %multiply_subtract_fusion.1) | copy-start | bytes 3145732
  532.6 7.1 collective-permute-start.8
  541.6 8.9 %copy-start.12 = (f32[1,4,256,512]{3,2,1,0:T(8,128)}, f32[1,4,256,512]{3,2,1,0:T(8,128)S(1)}, u32[]{:S(2)}) copy-start(f32[1,4,256,512]{3,2,1,0:T(8,128)S(1)} %fusion.36) | copy-start | bytes 6291460
  541.6 8.9 %collective-permute-start.9 = (f32[1,1,256,256]{3,2,1,0:T(8,128)S(1)}, f32[1,1,256,256]{3,2,1,0:T(8,128)S(1)}, u32[]{:S(2)}, u32[]{:S(2)}) collective-permute-start(f32[1,1,256,256]{3,2,1,0:T(8,128)S(1)} %slice.144), channel_id=1, source_target_pairs={{8,0},{16,8},{24,16},{32,24},{40,32},{48,40},{56,48},{64,56},{72,6... | collective-permute-start | bytes 786440 | tf_op jit(solution)/shard_map/ppermute | solution.py:13
  621.1 7.2 collective-permute-start.10
  634.1 102.6 %all-reduce.9.cloned.1.call-start = ((), (), s32[]{:S(2)}) async-start(), calls=%async_computation.8 | async-start | bytes 4194304 | tf_op jit(solution)/shard_map/psum | solution.py:79
  743.6 7.1 collective-permute-start.11
  (28 other events, 135.8 us)
Sparse Core Ops, SparseCore 0:
  42.1 38.4 reduce-scatter.3
  85.7 65.4 all-reduce.4
  341.8 31.8 reduce-scatter.5
  378.8 65.5 all-reduce.6
  634.2 31.8 reduce-scatter.7
  671.1 65.4 all-reduce.8
where the time goes:
time: 841 us; the launch traced here: 833 us
  waiting for transfers between devices  366 us (44%)
  blocking collectives  348 us (41%)
  matrix products  57.2 us (7%)
  starting transfers between devices  25.7 us (3%)
  other arithmetic  16.7 us (2%)
  between operations  15.2 us (2%)
    psum x3, blocking collectives, residual_sum(): return lax.psum(inner(resid, precond), ('sub', 'grp'))  206 us
    psum x3, waiting for transfers between devices, local(): solved = lax.psum(partial_solved, 'grp')  197 us
    psum x2, blocking collectives, local(): alpha = rz_now / lax.psum(inner(direction, image), ('sub', 'grp'))  142 us
    reduce_scatter x3, waiting for transfers between devices, local(): lax.psum_scatter(jnp.einsum('skn,srk->nr', corner_onehot, corner_vals, pr...  102 us
    ppermute x12, waiting for transfers between devices, passed_along(): return lax.ppermute(block, axis, route)  66.6 us
    ppermute x12, starting transfers between devices, passed_along(): return lax.ppermute(block, axis, route)  25.1 us
  transfers between devices with their start and end apart: 18, of which 18 were waited for; matrix products, arithmetic and copies ran while one was open for 0% of the time, Pallas kernels for 0%

commit v1 on v0

--- a/solution.py
+++ b/solution.py
@@ -41,7 +41,7 @@
 
 
 def residual_sum(resid, precond):
-    return lax.psum(inner(resid, precond), ("sub", "grp"))
+    return lax.psum(lax.psum(inner(resid, precond), "sub"), "grp")
 
 
 def local(rhs, counts, solve_panel, dirichlet_panel, coupling, corner_map, coarse_inverse):

time: 841 us -> 851 us (1.012)
  blocking collectives: 348 us -> 366 us
    psum x2 -> x3, blocking collectives: 142 us -> 212 us  [local(): alpha = rz_now / lax.psum(inner(direction, image), ('sub', 'grp'))]
    psum x3 -> x6, blocking collectives: 206 us -> 153 us  [residual_sum(): return lax.psum(lax.psum(inner(resid, precond), 'sub'), 'grp')]
where the time goes in v1:
time: 851 us; the launch traced here: 844 us
  blocking collectives  366 us (43%)
  waiting for transfers between devices  361 us (42%)
  matrix products  57.2 us (7%)
  starting transfers between devices  23.4 us (3%)
  other arithmetic  16.7 us (2%)
  between operations  15.4 us (2%)
    psum x3, blocking collectives, local(): alpha = rz_now / lax.psum(inner(direction, image), ('sub', 'grp'))  212 us
    psum x3, waiting for transfers between devices, local(): solved = lax.psum(partial_solved, 'grp')  197 us
    psum x6, blocking collectives, residual_sum(): return lax.psum(lax.psum(inner(resid, precond), 'sub'), 'grp')  153 us
    reduce_scatter x3, waiting for transfers between devices, local(): lax.psum_scatter(jnp.einsum('skn,srk->nr', corner_onehot, corner_vals, pr...  96.2 us
    ppermute x12, waiting for transfers between devices, passed_along(): return lax.ppermute(block, axis, route)  68.3 us
    ppermute x12, starting transfers between devices, passed_along(): return lax.ppermute(block, axis, route)  22.4 us
  transfers between devices with their start and end apart: 18, of which 18 were waited for; matrix products, arithmetic and copies ran while one was open for 0% of the time, Pallas kernels for 0%

profile of v1, /device:TPU:1, one launch (start us, length us, event | category | flops | bytes accessed | tf_op | source)
XLA Modules:
  0.0 843.9 jit_solution(2750090977817290234)
XLA Ops:
  21.7 7.8 collective-permute-done.1
  42.1 38.5 %reduce-scatter.4.cloned.1.call-done = f32[256,256]{1,0:T(8,128)} async-done(((f32[2048,256]{1,0:T(8,128)}), f32[256,256]{1,0:T(8,128)}) %reduce-scatter.4.cloned.1.call-update) | async-done | bytes 262160 | tf_op jit(solution)/shard_map/reduce_scatter | solution.py:72
  80.5 4.9 convolution_bitcast_fusion.5
  86.0 65.2 %all-reduce.4.cloned.1.call-done = f32[2048,256]{0,1:T(8,128)} async-done(((f32[2048,256]{0,1:T(8,128)}), f32[2048,256]{0,1:T(8,128)}) %all-reduce.4.cloned.1.call-update) | async-done | bytes 2097168 | tf_op jit(solution)/shard_map/psum | solution.py:79
  159.8 5.7 collective-permute-done.3
  166.2 70.6 %psum.87 = f32[256]{0:T(256)S(1)} all-reduce(f32[256]{0:T(256)S(1)} %get-tuple-element.2), channel_id=1, replica_groups=mesh['sub'=16,'grp'=8] {'sub','grp'}, use_global_device_ids=true, to_apply=%region_6.0 | all-reduce | flops 256 | bytes 2048 | tf_op jit(solution)/shard_map/psum | solution.py:86
  236.8 30.8 %psum.84 = f32[256]{0:T(256)S(1)} all-reduce(f32[256]{0:T(256)S(1)} %get-tuple-element.3), channel_id=1, replica_groups=mesh['sub'=16,'grp'=8] {'sub'}, use_global_device_ids=true, to_apply=%region_1.0 | all-reduce | flops 256 | bytes 2048 | tf_op jit(solution)/shard_map/psum | solution.py:44
  267.7 19.6 %psum.85 = f32[256]{0:T(256)S(1)} all-reduce(f32[256]{0:T(256)S(1)} %psum.84), channel_id=1, replica_groups=mesh['sub'=16,'grp'=8] {'grp'}, use_global_device_ids=true, to_apply=%region_2.0 | all-reduce | flops 256 | bytes 2048 | tf_op jit(solution)/shard_map/psum | solution.py:44
  290.9 5.2 collective-permute-done.4
  299.4 8.2 collective-permute-done.5
  308.6 29.7 %psum.88 = f32[256]{0:T(256)S(1)} all-reduce(f32[256]{0:T(256)S(1)} %multiply_reduce_fusion.3), channel_id=1, replica_groups=mesh['sub'=16,'grp'=8] {'sub'}, use_global_device_ids=true, to_apply=%region_8.0 | all-reduce | flops 256 | bytes 2048 | tf_op jit(solution)/shard_map/psum | solution.py:44
  338.3 21.1 %psum.89 = f32[256]{0:T(256)S(1)} all-reduce(f32[256]{0:T(256)S(1)} %psum.88), channel_id=1, replica_groups=mesh['sub'=16,'grp'=8] {'grp'}, use_global_device_ids=true, to_apply=%region_9.0 | all-reduce | flops 256 | bytes 2048 | tf_op jit(solution)/shard_map/psum | solution.py:44
  375.1 27.7 %reduce-scatter.6.cloned.1.call-done = f32[256,256]{1,0:T(8,128)} async-done(((f32[2048,256]{1,0:T(8,128)}), f32[256,256]{1,0:T(8,128)}) %reduce-scatter.6.cloned.1.call-update) | async-done | bytes 262160 | tf_op jit(solution)/shard_map/reduce_scatter | solution.py:72
  407.8 65.6 %all-reduce.6.cloned.1.call-done = f32[2048,256]{0,1:T(8,128)} async-done(((f32[2048,256]{0,1:T(8,128)}), f32[2048,256]{0,1:T(8,128)}) %all-reduce.6.cloned.1.call-update) | async-done | bytes 2097168 | tf_op jit(solution)/shard_map/psum | solution.py:79
  481.7 5.7 collective-permute-done.7
  488.4 70.9 %psum.91 = f32[256]{0:T(256)S(1)} all-reduce(f32[256]{0:T(256)S(1)} %multiply_reduce_fusion.2), channel_id=1, replica_groups=mesh['sub'=16,'grp'=8] {'sub','grp'}, use_global_device_ids=true, to_apply=%region_13.0 | all-reduce | flops 256 | bytes 2048 | tf_op jit(solution)/shard_map/psum | solution.py:86
  571.9 7.5 collective-permute-done.9
  580.5 30.7 %psum.92 = f32[256]{0:T(256)S(1)} all-reduce(f32[256]{0:T(256)S(1)} %multiply_reduce_fusion.1), channel_id=1, replica_groups=mesh['sub'=16,'grp'=8] {'sub'}, use_global_device_ids=true, to_apply=%region_15.0 | all-reduce | flops 256 | bytes 2048 | tf_op jit(solution)/shard_map/psum | solution.py:44
  611.2 21.4 %psum.93 = f32[256]{0:T(256)S(1)} all-reduce(f32[256]{0:T(256)S(1)} %psum.92), channel_id=1, replica_groups=mesh['sub'=16,'grp'=8] {'grp'}, use_global_device_ids=true, to_apply=%region_16.0 | all-reduce | flops 256 | bytes 2048 | tf_op jit(solution)/shard_map/psum | solution.py:44
  635.8 5.0 collective-permute-done.10
  646.8 30.1 %reduce-scatter.8.cloned.1.call-done = f32[256,256]{1,0:T(8,128)} async-done(((f32[2048,256]{1,0:T(8,128)}), f32[256,256]{1,0:T(8,128)}) %reduce-scatter.8.cloned.1.call-update) | async-done | bytes 262160 | tf_op jit(solution)/shard_map/reduce_scatter | solution.py:72
  681.8 65.8 %all-reduce.8.cloned.1.call-done = f32[2048,256]{0,1:T(8,128)} async-done(((f32[2048,256]{0,1:T(8,128)}), f32[2048,256]{0,1:T(8,128)}) %all-reduce.8.cloned.1.call-update) | async-done | bytes 2097168 | tf_op jit(solution)/shard_map/psum | solution.py:79
  755.8 5.7 collective-permute-done.11
  761.8 70.7 %psum.95 = f32[256]{0:T(256)S(1)} all-reduce(f32[256]{0:T(256)S(1)} %multiply_reduce_fusion), channel_id=1, replica_groups=mesh['sub'=16,'grp'=8] {'sub','grp'}, use_global_device_ids=true, to_apply=%region_20.0 | all-reduce | flops 256 | bytes 2048 | tf_op jit(solution)/shard_map/psum | solution.py:86
  (165 shorter events, 114.3 us)
Async XLA Ops:
  7.2 11.3 %copy-start = (bf16[1,4,512,512]{3,2,1,0:T(8,128)(2,1)S(1)}, bf16[1,4,512,512]{3,2,1,0:T(8,128)(2,1)}, u32[]{:S(2)}) copy-start(bf16[1,4,512,512]{3,2,1,0:T(8,128)(2,1)} %param.10) | copy-start | bytes 6291460
  7.2 73.4 %reduce-scatter.4.cloned.1.call-start = ((), (), s32[]{:S(2)}) async-start(), calls=%async_computation.3 | async-start | bytes 2359296 | tf_op jit(solution)/shard_map/reduce_scatter | solution.py:72
  9.4 8.9 %collective-permute-start = (f32[1,1,256,256]{3,2,1,0:T(8,128)S(1)}, f32[1,1,256,256]{3,2,1,0:T(8,128)S(1)}, u32[]{:S(2)}, u32[]{:S(2)}) collective-permute-start(f32[1,1,256,256]{3,2,1,0:T(8,128)S(1)} %slice.120), channel_id=1, source_target_pairs={{0,8},{8,16},{16,24},{24,32},{32,40},{40,48},{48,56},{56,64},{64,7... | collective-permute-start | bytes 786440 | tf_op jit(solution)/shard_map/ppermute | solution.py:13
  20.3 9.2 %collective-permute-start.1 = (f32[1,1,256,256]{3,2,1,0:T(8,128)S(1)}, f32[1,1,256,256]{3,2,1,0:T(8,128)S(1)}, u32[]{:S(2)}, u32[]{:S(2)}) collective-permute-start(f32[1,1,256,256]{3,2,1,0:T(8,128)S(1)} %slice.124), channel_id=1, source_target_pairs={{8,0},{16,8},{24,16},{32,24},{40,32},{48,40},{56,48},{64,56},{72,6... | collective-permute-start | bytes 786440 | tf_op jit(solution)/shard_map/ppermute | solution.py:13
  29.7 135.8 %copy-start.8 = (f32[1,4,256,256]{3,2,1,0:T(8,128)}, f32[1,4,256,256]{3,2,1,0:T(8,128)S(1)}, u32[]{:S(2)}) copy-start(f32[1,4,256,256]{3,2,1,0:T(8,128)S(1)} %get-tuple-element.7) | copy-start | bytes 3145732
  29.8 6.5 collective-permute-start.2
  42.0 109.2 %all-reduce.4.cloned.1.call-start = ((), (), s32[]{:S(2)}) async-start(), calls=%async_computation.4 | async-start | bytes 4194304 | tf_op jit(solution)/shard_map/psum | solution.py:79
  85.5 317.3 %reduce-scatter.6.cloned.1.call-start = ((), (), s32[]{:S(2)}) async-start(), calls=%async_computation.5 | async-start | bytes 2359296 | tf_op jit(solution)/shard_map/reduce_scatter | solution.py:72
  158.1 7.4 collective-permute-start.3
  289.4 18.2 %copy-start.4 = (f32[1,4,256,256]{3,2,1,0:T(8,128)}, f32[1,4,256,256]{3,2,1,0:T(8,128)S(1)}, u32[]{:S(2)}) copy-start(f32[1,4,256,256]{3,2,1,0:T(8,128)S(1)} %multiply_subtract_fusion.2) | copy-start | bytes 3145732
  289.5 6.6 collective-permute-start.4
  298.0 9.6 %copy-start.11 = (f32[1,4,256,512]{3,2,1,0:T(8,128)}, f32[1,4,256,512]{3,2,1,0:T(8,128)S(1)}, u32[]{:S(2)}) copy-start(f32[1,4,256,512]{3,2,1,0:T(8,128)S(1)} %fusion.39) | copy-start | bytes 6291460
  298.0 9.5 %collective-permute-start.5 = (f32[1,1,256,256]{3,2,1,0:T(8,128)S(1)}, f32[1,1,256,256]{3,2,1,0:T(8,128)S(1)}, u32[]{:S(2)}, u32[]{:S(2)}) collective-permute-start(f32[1,1,256,256]{3,2,1,0:T(8,128)S(1)} %slice.134), channel_id=1, source_target_pairs={{8,0},{16,8},{24,16},{32,24},{40,32},{48,40},{56,48},{64,56},{72,6... | collective-permute-start | bytes 786440 | tf_op jit(solution)/shard_map/ppermute | solution.py:13
  361.5 6.9 collective-permute-start.6
  375.1 98.3 %all-reduce.6.cloned.1.call-start = ((), (), s32[]{:S(2)}) async-start(), calls=%async_computation.6 | async-start | bytes 4194304 | tf_op jit(solution)/shard_map/psum | solution.py:79
  407.7 269.1 %reduce-scatter.8.cloned.1.call-start = ((), (), s32[]{:S(2)}) async-start(), calls=%async_computation.7 | async-start | bytes 2359296 | tf_op jit(solution)/shard_map/reduce_scatter | solution.py:72
  480.3 7.1 collective-permute-start.7
  561.4 18.0 %copy-start.3 = (f32[1,4,256,256]{3,2,1,0:T(8,128)}, f32[1,4,256,256]{3,2,1,0:T(8,128)S(1)}, u32[]{:S(2)}) copy-start(f32[1,4,256,256]{3,2,1,0:T(8,128)S(1)} %multiply_subtract_fusion.1) | copy-start | bytes 3145732
  561.4 7.1 collective-permute-start.8
  570.5 8.9 %copy-start.12 = (f32[1,4,256,512]{3,2,1,0:T(8,128)}, f32[1,4,256,512]{3,2,1,0:T(8,128)S(1)}, u32[]{:S(2)}) copy-start(f32[1,4,256,512]{3,2,1,0:T(8,128)S(1)} %fusion.36) | copy-start | bytes 6291460
  570.5 8.9 %collective-permute-start.9 = (f32[1,1,256,256]{3,2,1,0:T(8,128)S(1)}, f32[1,1,256,256]{3,2,1,0:T(8,128)S(1)}, u32[]{:S(2)}, u32[]{:S(2)}) collective-permute-start(f32[1,1,256,256]{3,2,1,0:T(8,128)S(1)} %slice.144), channel_id=1, source_target_pairs={{8,0},{16,8},{24,16},{32,24},{40,32},{48,40},{56,48},{64,56},{72,6... | collective-permute-start | bytes 786440 | tf_op jit(solution)/shard_map/ppermute | solution.py:13
  634.4 6.4 collective-permute-start.10
  646.5 101.1 %all-reduce.8.cloned.1.call-start = ((), (), s32[]{:S(2)}) async-start(), calls=%async_computation.8 | async-start | bytes 4194304 | tf_op jit(solution)/shard_map/psum | solution.py:79
  754.4 7.1 collective-permute-start.11
  (28 other events, 135.6 us)
Sparse Core Ops, SparseCore 0:
  42.1 38.3 reduce-scatter.3
  85.6 65.6 all-reduce.3
  375.2 27.5 reduce-scatter.5
  407.8 65.5 all-reduce.5
  646.6 30.2 reduce-scatter.7
  681.9 65.5 all-reduce.7
